TPU v7x, 512 devices: a whole 4x8x8 slice. The times are simulated.
512 devices in a mesh: pa: 8 (over y), pb: 64 (over z, x, core).
Axes of the slice: x: 4, y: 8, z: 8, core: 2. Of those that a mesh axis runs over, the one named last changes fastest.
Arguments:
- matrix: bfloat16 [12288, 24576], P('pa', 'pb'), may hold values from -6 to 6
- panels: bfloat16 [6, 12288, 128], P(None, ('pa', 'pb')), may hold values from -0.25 to 0.25
- inverses: float32 [6, 128, 128], replicated, as said below
- pivots: int32 [6, 128], replicated, may hold values from 128 to 12287, as said below
Outputs:
- factored: bfloat16 [12288, 24576], P('pa', 'pb')
Inputs may be any that keep to these rules, and one draw needn't show every extreme that they name: `pivots`: row k lists 128 different row numbers, each at least (k + 1) * 128. `inverses`: each block is unit lower triangular.
All inputs are finite; a program needn't handle non-finite values.
Results may differ from a plain program's by a relative error of at most 0.0082.
Values may be sent and summed in bfloat16 or wider, within the bound.
No kernel may reach another device: no remote copies, remote signals or barrier semaphores. Data moves between devices by JAX's collectives and lax.ppermute only.
A program may use at most 64 MiB of HBM per device.

v0:
```python
import jax
import jax.numpy as jnp
from jax import lax
from jax.sharding import PartitionSpec as P

NB = 128
STEPS = 6


def broadcast(x, axis, root):
    mine = lax.axis_index(axis) == root
    return lax.psum(jnp.where(mine, x, jnp.zeros_like(x)), axis)


def per_device(matrix, panels, inverses, pivots):
    local_rows = matrix.shape[0]
    proc_row = lax.axis_index("pa")
    first_row = proc_row * local_rows
    is_owner = proc_row == 0
    global_rows = first_row + jnp.arange(local_rows, dtype=jnp.int32)
    for step in range(STEPS):
        lo = step * NB
        hi = lo + NB
        chosen = pivots[step]
        local_idx = chosen - first_row
        owned = (local_idx >= 0) & (local_idx < local_rows)
        safe_idx = jnp.clip(local_idx, 0, local_rows - 1)
        candidates = jnp.where(
            owned[:, None], jnp.take(matrix, safe_idx, axis=0), jnp.zeros((), jnp.bfloat16)
        )
        top_local = matrix[lo:hi]
        new_top = lax.psum(candidates, "pa").astype(jnp.float32).astype(jnp.bfloat16)
        upper_here = jnp.dot(
            inverses[step],
            new_top.astype(jnp.float32),
            precision=lax.Precision.HIGHEST,
            preferred_element_type=jnp.float32,
        ).astype(jnp.bfloat16)
        upper, old_top = (broadcast(upper_here, "pa", 0), broadcast(top_local, "pa", 0))
        target = jnp.where(owned, local_idx, local_rows)
        matrix = matrix.at[target].set(old_top, mode="drop")
        product = jnp.dot(
            lax.all_gather(panels[step], "pb", axis=0, tiled=True),
            upper,
            preferred_element_type=jnp.float32,
        )
        updated = (matrix.astype(jnp.float32) - product).astype(jnp.bfloat16)
        matrix = jnp.where((global_rows >= hi)[:, None], updated, matrix)
        matrix = matrix.at[lo:hi].set(jnp.where(is_owner, upper, matrix[lo:hi]))
    return matrix


def solution(mesh):
    in_specs = (P("pa", "pb"), P(None, ("pa", "pb"), None), P(), P())
    out_specs = P("pa", "pb")
    return jax.shard_map(
        per_device, mesh=mesh, in_specs=in_specs, out_specs=out_specs, check_vma=False
    )
```

profile of v0, /device:TPU:2, one launch (start us, length us, event | category | flops | bytes accessed | tf_op | source)
XLA Modules:
  0.0 992.1 jit_solution(16481884863507782826)
XLA Ops:
  15.7 57.5 %all-gather = bf16[1,1536,128]{2,1,0:T(8,128)(2,1)} all-gather(bf16[1,24,128]{2,1,0:T(8,128)(2,1)S(1)} %get-tuple-element.106), channel_id=2, replica_groups=mesh['pa'=8,'pb'=64] {'pb'}, dimensions={1}, use_global_device_ids=true | all-gather | bytes 399360 | tf_op jit(solution)/shard_map/all_gather | solution.py:43
  73.2 19.3 %all-reduce.19.cloned.1.call-done = bf16[128,384]{0,1:T(8,128)(2,1)} async-done(((bf16[128,384]{0,1:T(8,128)(2,1)}), bf16[128,384]{0,1:T(8,128)(2,1)}) %all-reduce.19.cloned.1.call-update) | async-done | bytes 98320 | tf_op jit(solution)/shard_map/psum | solution.py:32
  92.5 1.8 fusion.19
  95.0 75.9 %all-reduce.41.cloned.1.call-done = (bf16[128,384]{0,1:T(8,128)(2,1)}, bf16[128,384]{0,1:T(8,128)(2,1)}) async-done(((bf16[128,384]{0,1:T(8,128)(2,1)}, bf16[128,384]{0,1:T(8,128)(2,1)}), (bf16[128,384]{0,1:T(8,128)(2,1)}, bf16[128,384]{0,1:T(8,128)(2,1)})) %all-reduce.41.cloned.1.call-update) | async-done | bytes 196624 | tf_op jit(solution)/shard_map/psum | solution.py:12
  171.9 1.7 scatter_fusion
  174.3 1.5 fusion.17
  179.2 75.1 %all-reduce.21.cloned.1.call-done = bf16[128,384]{0,1:T(8,128)(2,1)} async-done(((bf16[128,384]{0,1:T(8,128)(2,1)}), bf16[128,384]{0,1:T(8,128)(2,1)}) %all-reduce.21.cloned.1.call-update) | async-done | bytes 98320 | tf_op jit(solution)/shard_map/psum | solution.py:32
  254.4 1.8 fusion.21
  256.2 53.6 %all-gather.1 = bf16[1,1536,128]{2,1,0:T(8,128)(2,1)} all-gather(bf16[1,24,128]{2,1,0:T(8,128)(2,1)S(1)} %copy-done.9), channel_id=3, replica_groups=mesh['pa'=8,'pb'=64] {'pb'}, dimensions={1}, use_global_device_ids=true | all-gather | bytes 399360 | tf_op jit(solution)/shard_map/all_gather | solution.py:43
  310.5 22.2 %all-reduce.39.cloned.1.call-done = (bf16[128,384]{0,1:T(8,128)(2,1)}, bf16[128,384]{0,1:T(8,128)(2,1)}) async-done(((bf16[128,384]{0,1:T(8,128)(2,1)}, bf16[128,384]{0,1:T(8,128)(2,1)}), (bf16[128,384]{0,1:T(8,128)(2,1)}, bf16[128,384]{0,1:T(8,128)(2,1)})) %all-reduce.39.cloned.1.call-update) | async-done | bytes 196624 | tf_op jit(solution)/shard_map/psum | solution.py:12
  333.6 1.7 scatter_fusion.1
  341.0 75.2 %all-reduce.23.cloned.1.call-done = bf16[128,384]{0,1:T(8,128)(2,1)} async-done(((bf16[128,384]{0,1:T(8,128)(2,1)}), bf16[128,384]{0,1:T(8,128)(2,1)}) %all-reduce.23.cloned.1.call-update) | async-done | bytes 98320 | tf_op jit(solution)/shard_map/psum | solution.py:32
  416.1 1.8 fusion.23
  418.0 53.8 %all-gather.2 = bf16[1,1536,128]{2,1,0:T(8,128)(2,1)} all-gather(bf16[1,24,128]{2,1,0:T(8,128)(2,1)S(1)} %copy-done.8), channel_id=4, replica_groups=mesh['pa'=8,'pb'=64] {'pb'}, dimensions={1}, use_global_device_ids=true | all-gather | bytes 399360 | tf_op jit(solution)/shard_map/all_gather | solution.py:43
  472.4 22.0 %all-reduce.37.cloned.1.call-done = (bf16[128,384]{0,1:T(8,128)(2,1)}, bf16[128,384]{0,1:T(8,128)(2,1)}) async-done(((bf16[128,384]{0,1:T(8,128)(2,1)}, bf16[128,384]{0,1:T(8,128)(2,1)}), (bf16[128,384]{0,1:T(8,128)(2,1)}, bf16[128,384]{0,1:T(8,128)(2,1)})) %all-reduce.37.cloned.1.call-update) | async-done | bytes 196624 | tf_op jit(solution)/shard_map/psum | solution.py:12
  495.4 1.7 scatter_fusion.2
  502.7 75.2 %all-reduce.25.cloned.1.call-done = bf16[128,384]{0,1:T(8,128)(2,1)} async-done(((bf16[128,384]{0,1:T(8,128)(2,1)}), bf16[128,384]{0,1:T(8,128)(2,1)}) %all-reduce.25.cloned.1.call-update) | async-done | bytes 98320 | tf_op jit(solution)/shard_map/psum | solution.py:32
  577.9 1.8 fusion.25
  579.7 53.6 %all-gather.3 = bf16[1,1536,128]{2,1,0:T(8,128)(2,1)} all-gather(bf16[1,24,128]{2,1,0:T(8,128)(2,1)S(1)} %copy-done.7), channel_id=5, replica_groups=mesh['pa'=8,'pb'=64] {'pb'}, dimensions={1}, use_global_device_ids=true | all-gather | bytes 399360 | tf_op jit(solution)/shard_map/all_gather | solution.py:43
  633.9 22.3 %all-reduce.35.cloned.1.call-done = (bf16[128,384]{0,1:T(8,128)(2,1)}, bf16[128,384]{0,1:T(8,128)(2,1)}) async-done(((bf16[128,384]{0,1:T(8,128)(2,1)}, bf16[128,384]{0,1:T(8,128)(2,1)}), (bf16[128,384]{0,1:T(8,128)(2,1)}, bf16[128,384]{0,1:T(8,128)(2,1)})) %all-reduce.35.cloned.1.call-update) | async-done | bytes 196624 | tf_op jit(solution)/shard_map/psum | solution.py:12
  657.3 1.7 scatter_fusion.3
  664.6 75.1 %all-reduce.27.cloned.1.call-done = bf16[128,384]{0,1:T(8,128)(2,1)} async-done(((bf16[128,384]{0,1:T(8,128)(2,1)}), bf16[128,384]{0,1:T(8,128)(2,1)}) %all-reduce.27.cloned.1.call-update) | async-done | bytes 98320 | tf_op jit(solution)/shard_map/psum | solution.py:32
  739.7 1.8 fusion.27
  741.6 53.8 %all-gather.4 = bf16[1,1536,128]{2,1,0:T(8,128)(2,1)} all-gather(bf16[1,24,128]{2,1,0:T(8,128)(2,1)S(1)} %get-tuple-element.107), channel_id=6, replica_groups=mesh['pa'=8,'pb'=64] {'pb'}, dimensions={1}, use_global_device_ids=true | all-gather | bytes 399360 | tf_op jit(solution)/shard_map/all_gather | solution.py:43
  795.4 22.5 %all-reduce.33.cloned.1.call-done = (bf16[128,384]{0,1:T(8,128)(2,1)}, bf16[128,384]{0,1:T(8,128)(2,1)}) async-done(((bf16[128,384]{0,1:T(8,128)(2,1)}, bf16[128,384]{0,1:T(8,128)(2,1)}), (bf16[128,384]{0,1:T(8,128)(2,1)}, bf16[128,384]{0,1:T(8,128)(2,1)})) %all-reduce.33.cloned.1.call-update) | async-done | bytes 196624 | tf_op jit(solution)/shard_map/psum | solution.py:12
  819.0 1.7 scatter_fusion.4
  821.4 1.5 fusion.13
  826.2 75.2 %all-reduce.29.cloned.1.call-done = bf16[128,384]{0,1:T(8,128)(2,1)} async-done(((bf16[128,384]{0,1:T(8,128)(2,1)}), bf16[128,384]{0,1:T(8,128)(2,1)}) %all-reduce.29.cloned.1.call-update) | async-done | bytes 98320 | tf_op jit(solution)/shard_map/psum | solution.py:32
  901.4 1.8 fusion.29
  903.2 49.0 %all-gather.5 = bf16[1,1536,128]{2,1,0:T(8,128)(2,1)S(1)} all-gather(bf16[1,24,128]{2,1,0:T(8,128)(2,1)S(1)} %get-tuple-element.102), channel_id=7, replica_groups=mesh['pa'=8,'pb'=64] {'pb'}, dimensions={1}, use_global_device_ids=true | all-gather | bytes 399360 | tf_op jit(solution)/shard_map/all_gather | solution.py:43
  952.2 27.4 %all-reduce.31.cloned.1.call-done = (bf16[128,384]{0,1:T(8,128)(2,1)}, bf16[128,384]{0,1:T(8,128)(2,1)}) async-done(((bf16[128,384]{0,1:T(8,128)(2,1)}, bf16[128,384]{0,1:T(8,128)(2,1)}), (bf16[128,384]{0,1:T(8,128)(2,1)}, bf16[128,384]{0,1:T(8,128)(2,1)})) %all-reduce.31.cloned.1.call-update) | async-done | bytes 196624 | tf_op jit(solution)/shard_map/psum | solution.py:12
  980.6 1.7 scatter_fusion.5
  (157 shorter events, 44.9 us)
Async XLA Ops:
  6.5 86.0 %all-reduce.19.cloned.1.call-start = ((), (), s32[]{:S(2)}) async-start(), calls=%async_computation | async-start | bytes 196608 | tf_op jit(solution)/shard_map/psum | solution.py:32
  7.8 5.5 copy-start.6
  10.7 160.2 %all-reduce.41.cloned.1.call-start = ((), (), s32[]{:S(2)}) async-start(), calls=%async_computation.11 | async-start | bytes 393216 | tf_op jit(solution)/shard_map/psum | solution.py:12
  94.3 160.1 %all-reduce.21.cloned.1.call-start = ((), (), s32[]{:S(2)}) async-start(), calls=%async_computation.1 | async-start | bytes 196608 | tf_op jit(solution)/shard_map/psum | solution.py:32
  175.9 1.9 copy-start.16
  175.9 1.9 copy-start.25
  176.7 79.5 %copy-start.9 = (bf16[1,24,128]{2,1,0:T(8,128)(2,1)S(1)}, bf16[1,24,128]{2,1,0:T(8,128)(2,1)}, u32[]{:S(2)}) copy-start(bf16[1,24,128]{2,1,0:T(8,128)(2,1)} %get-tuple-element.105) | copy-start | bytes 18436
  176.7 133.2 %copy-start.30 = (s32[128]{0:T(128)S(1)}, s32[128]{0:T(128)}, u32[]{:S(2)}) copy-start(s32[128]{0:T(128)} %get-tuple-element.119) | copy-start | bytes 1540
  176.7 156.9 %copy-start.26 = (s32[128]{0:T(128)S(1)}, s32[128]{0:T(128)}, u32[]{:S(2)}) copy-start(s32[128]{0:T(128)} %get-tuple-element.125) | copy-start | bytes 1540
  178.5 154.1 %all-reduce.39.cloned.1.call-start = ((), (), s32[]{:S(2)}) async-start(), calls=%async_computation.10 | async-start | bytes 393216 | tf_op jit(solution)/shard_map/psum | solution.py:12
  256.2 159.9 %all-reduce.23.cloned.1.call-start = ((), (), s32[]{:S(2)}) async-start(), calls=%async_computation.2 | async-start | bytes 196608 | tf_op jit(solution)/shard_map/psum | solution.py:32
  337.7 1.9 copy-start.15
  337.7 1.9 copy-start.23
  338.4 79.5 %copy-start.8 = (bf16[1,24,128]{2,1,0:T(8,128)(2,1)S(1)}, bf16[1,24,128]{2,1,0:T(8,128)(2,1)}, u32[]{:S(2)}) copy-start(bf16[1,24,128]{2,1,0:T(8,128)(2,1)} %get-tuple-element.104) | copy-start | bytes 18436
  338.4 133.3 %copy-start.29 = (s32[128]{0:T(128)S(1)}, s32[128]{0:T(128)}, u32[]{:S(2)}) copy-start(s32[128]{0:T(128)} %get-tuple-element.117) | copy-start | bytes 1540
  338.5 156.9 %copy-start.24 = (s32[128]{0:T(128)S(1)}, s32[128]{0:T(128)}, u32[]{:S(2)}) copy-start(s32[128]{0:T(128)} %get-tuple-element.126) | copy-start | bytes 1540
  340.3 154.1 %all-reduce.37.cloned.1.call-start = ((), (), s32[]{:S(2)}) async-start(), calls=%async_computation.9 | async-start | bytes 393216 | tf_op jit(solution)/shard_map/psum | solution.py:12
  417.9 159.9 %all-reduce.25.cloned.1.call-start = ((), (), s32[]{:S(2)}) async-start(), calls=%async_computation.3 | async-start | bytes 196608 | tf_op jit(solution)/shard_map/psum | solution.py:32
  499.4 1.9 copy-start.14
  499.4 1.9 copy-start.21
  500.2 79.5 %copy-start.7 = (bf16[1,24,128]{2,1,0:T(8,128)(2,1)S(1)}, bf16[1,24,128]{2,1,0:T(8,128)(2,1)}, u32[]{:S(2)}) copy-start(bf16[1,24,128]{2,1,0:T(8,128)(2,1)} %get-tuple-element.103) | copy-start | bytes 18436
  500.2 133.2 %copy-start.28 = (s32[128]{0:T(128)S(1)}, s32[128]{0:T(128)}, u32[]{:S(2)}) copy-start(s32[128]{0:T(128)} %get-tuple-element.115) | copy-start | bytes 1540
  500.2 157.1 %copy-start.22 = (s32[128]{0:T(128)S(1)}, s32[128]{0:T(128)}, u32[]{:S(2)}) copy-start(s32[128]{0:T(128)} %get-tuple-element.127) | copy-start | bytes 1540
  502.0 154.2 %all-reduce.35.cloned.1.call-start = ((), (), s32[]{:S(2)}) async-start(), calls=%async_computation.8 | async-start | bytes 393216 | tf_op jit(solution)/shard_map/psum | solution.py:12
  579.7 160.1 %all-reduce.27.cloned.1.call-start = ((), (), s32[]{:S(2)}) async-start(), calls=%async_computation.4 | async-start | bytes 196608 | tf_op jit(solution)/shard_map/psum | solution.py:32
  661.3 1.9 copy-start.19
  662.1 133.4 %copy-start.27 = (s32[128]{0:T(128)S(1)}, s32[128]{0:T(128)}, u32[]{:S(2)}) copy-start(s32[128]{0:T(128)} %get-tuple-element.91) | copy-start | bytes 1540
  662.1 156.9 %copy-start.20 = (s32[128]{0:T(128)S(1)}, s32[128]{0:T(128)}, u32[]{:S(2)}) copy-start(s32[128]{0:T(128)} %get-tuple-element.128) | copy-start | bytes 1540
  663.9 154.1 %all-reduce.33.cloned.1.call-start = ((), (), s32[]{:S(2)}) async-start(), calls=%async_computation.7 | async-start | bytes 393216 | tf_op jit(solution)/shard_map/psum | solution.py:12
  741.5 159.8 %all-reduce.29.cloned.1.call-start = ((), (), s32[]{:S(2)}) async-start(), calls=%async_computation.5 | async-start | bytes 196608 | tf_op jit(solution)/shard_map/psum | solution.py:32
  823.8 156.8 %copy-start.18 = (s32[128]{0:T(128)S(1)}, s32[128]{0:T(128)}, u32[]{:S(2)}) copy-start(s32[128]{0:T(128)} %get-tuple-element.124) | copy-start | bytes 1540
  825.5 154.1 %all-reduce.31.cloned.1.call-start = ((), (), s32[]{:S(2)}) async-start(), calls=%async_computation.6 | async-start | bytes 393216 | tf_op jit(solution)/shard_map/psum | solution.py:12
  (11 other events, 16.0 us)
Sparse Core Ops, SparseCore 0:
  10.8 81.6 all-reduce.18
  95.0 75.9 all-reduce.40
  178.7 75.6 all-reduce.20
  256.7 75.9 all-reduce.38
  340.4 75.6 all-reduce.22
  418.4 75.9 all-reduce.36
  502.1 75.6 all-reduce.24
  580.3 75.9 all-reduce.34
  664.0 75.6 all-reduce.26
  742.0 75.9 all-reduce.32
  825.6 75.6 all-reduce.28
  903.7 75.9 all-reduce.30
where the time goes:
time: 993 us; the launch traced here: 992 us
  waiting for transfers between devices  588 us (59%)
  blocking collectives  321 us (32%)
  local copies, waits for them, and re-layouts  34.2 us (3%)
  matrix products  18.7 us (2%)
  other arithmetic  15.4 us (2%)
  between operations  14.3 us (1%)
    psum x6, waiting for transfers between devices, per_device(): lax.psum(candidates, 'pa').astype(jnp.float32).astype(jnp.bfloat16)  395 us
    all_gather x6, blocking collectives, per_device(): lax.all_gather(panels[step], 'pb', axis=0, tiled=True)  321 us
    psum x6, waiting for transfers between devices, broadcast(): return lax.psum(jnp.where(mine, x, jnp.zeros_like(x)), axis)  192 us
  transfers between devices with their start and end apart: 12, of which 12 were waited for; matrix products, arithmetic and copies ran while one was open for 1% of the time, Pallas kernels for 0%

commit v1 on v0

--- a/solution.py
+++ b/solution.py
@@ -5,6 +5,12 @@
 
 NB = 128
 STEPS = 6
+
+
+def lanes_take(across, inp):
+    return jnp.concatenate(
+        jax.lax.all_to_all(jnp.stack(jax.lax.axis_size(across) * [inp]), across, 0, 0), axis=0
+    )
 
 
 def broadcast(x, axis, root):
@@ -39,11 +45,7 @@
         upper, old_top = (broadcast(upper_here, "pa", 0), broadcast(top_local, "pa", 0))
         target = jnp.where(owned, local_idx, local_rows)
         matrix = matrix.at[target].set(old_top, mode="drop")
-        product = jnp.dot(
-            lax.all_gather(panels[step], "pb", axis=0, tiled=True),
-            upper,
-            preferred_element_type=jnp.float32,
-        )
+        product = jnp.dot(lanes_take("pb", panels[step]), upper, preferred_element_type=jnp.float32)
         updated = (matrix.astype(jnp.float32) - product).astype(jnp.bfloat16)
         matrix = jnp.where((global_rows >= hi)[:, None], updated, matrix)
         matrix = matrix.at[lo:hi].set(jnp.where(is_owner, upper, matrix[lo:hi]))

time: 993 us -> 1050 us (1.057)
  blocking collectives: 321 us -> 0 us
  waiting for transfers between devices: 588 us -> 892 us
  starting transfers between devices: 0.46 us -> 69.7 us
    all_gather x6 -> x0, blocking collectives: 321 us -> none  [per_device(): lax.all_gather(panels[step], 'pb', axis=0, tiled=True)]
    psum x6, waiting for transfers between devices: 192 us -> 455 us  [broadcast(): return lax.psum(jnp.where(mine, x, jnp.zeros_like(x)), axis)]
    all_to_all x0 -> x6, starting transfers between devices: none -> 69.2 us  [lanes_take(): jax.lax.all_to_all(jnp.stack(jax.lax.axis_size(across) * [inp]), across,...]
    psum x6, waiting for transfers between devices: 395 us -> 437 us  [per_device(): lax.psum(candidates, 'pa').astype(jnp.float32).astype(jnp.bfloat16)]
  transfers between devices with their start and end apart: 12 -> 18, of which waited for: 12 -> 12; matrix products, arithmetic and copies ran while one was open for 1% -> 6% of each run, Pallas kernels for 0% -> 0%
where the time goes in v1:
time: 1050 us
  waiting for transfers between devices  892 us (85%)
  starting transfers between devices  69.7 us (7%)
  local copies, waits for them, and re-layouts  39.2 us (4%)
  matrix products  19.6 us (2%)
  other arithmetic  15.1 us (1%)
  between operations  14.4 us (1%)
    psum x6, waiting for transfers between devices, broadcast(): return lax.psum(jnp.where(mine, x, jnp.zeros_like(x)), axis)  455 us
    psum x6, waiting for transfers between devices, per_device(): lax.psum(candidates, 'pa').astype(jnp.float32).astype(jnp.bfloat16)  437 us
    all_to_all x6, starting transfers between devices, lanes_take(): jax.lax.all_to_all(jnp.stack(jax.lax.axis_size(across) * [inp]), across,...  69.2 us
  transfers between devices with their start and end apart: 18, of which 12 were waited for; matrix products, arithmetic and copies ran while one was open for 6% of the time, Pallas kernels for 0%

profile of v1, /device:TPU:2, one launch (start us, length us, event | category | flops | bytes accessed | tf_op | source)
XLA Modules:
  0.0 1050.0 jit_solution(5168729202979254448)
XLA Ops:
  12.1 13.9 %all-to-all-start = ((bf16[64,24,128]{2,1,0:T(8,128)(2,1)}), bf16[64,24,128]{2,1,0:T(8,128)(2,1)S(1)}, u32[]{:S(2)}, u32[]{:S(2)}) async-start(bf16[64,24,128]{2,1,0:T(8,128)(2,1)} %stack.18), calls=%async_computation | async-start | bytes 786432 | tf_op jit(solution)/shard_map/all_to_all | solution.py:12
  28.1 64.5 %all-reduce.19.cloned.1.call-done = bf16[128,384]{0,1:T(8,128)(2,1)} async-done(((bf16[128,384]{0,1:T(8,128)(2,1)}), bf16[128,384]{0,1:T(8,128)(2,1)}) %all-reduce.19.cloned.1.call-update) | async-done | bytes 98320 | tf_op jit(solution)/shard_map/psum | solution.py:38
  92.5 1.8 fusion.19
  95.0 76.0 %all-reduce.41.cloned.1.call-done = (bf16[128,384]{0,1:T(8,128)(2,1)}, bf16[128,384]{0,1:T(8,128)(2,1)}) async-done(((bf16[128,384]{0,1:T(8,128)(2,1)}, bf16[128,384]{0,1:T(8,128)(2,1)}), (bf16[128,384]{0,1:T(8,128)(2,1)}, bf16[128,384]{0,1:T(8,128)(2,1)})) %all-reduce.41.cloned.1.call-update) | async-done | bytes 196624 | tf_op jit(solution)/shard_map/psum | solution.py:18
  171.9 1.7 scatter_fusion
  175.2 11.1 %all-to-all-start.1 = ((bf16[64,24,128]{2,1,0:T(8,128)(2,1)}), bf16[64,24,128]{2,1,0:T(8,128)(2,1)}, u32[]{:S(2)}, u32[]{:S(2)}) async-start(bf16[64,24,128]{2,1,0:T(8,128)(2,1)} %stack.19), calls=%async_computation.1 | async-start | bytes 786432 | tf_op jit(solution)/shard_map/all_to_all | solution.py:12
  186.3 1.5 fusion.17
  191.2 74.5 %all-reduce.21.cloned.1.call-done = bf16[128,384]{0,1:T(8,128)(2,1)} async-done(((bf16[128,384]{0,1:T(8,128)(2,1)}), bf16[128,384]{0,1:T(8,128)(2,1)}) %all-reduce.21.cloned.1.call-update) | async-done | bytes 98320 | tf_op jit(solution)/shard_map/psum | solution.py:38
  265.7 1.8 fusion.21
  268.8 75.2 %all-reduce.39.cloned.1.call-done = (bf16[128,384]{0,1:T(8,128)(2,1)}, bf16[128,384]{0,1:T(8,128)(2,1)}) async-done(((bf16[128,384]{0,1:T(8,128)(2,1)}, bf16[128,384]{0,1:T(8,128)(2,1)}), (bf16[128,384]{0,1:T(8,128)(2,1)}, bf16[128,384]{0,1:T(8,128)(2,1)})) %all-reduce.39.cloned.1.call-update) | async-done | bytes 196624 | tf_op jit(solution)/shard_map/psum | solution.py:18
  345.0 1.7 scatter_fusion.1
  348.2 11.1 %all-to-all-start.2 = ((bf16[64,24,128]{2,1,0:T(8,128)(2,1)}), bf16[64,24,128]{2,1,0:T(8,128)(2,1)}, u32[]{:S(2)}, u32[]{:S(2)}) async-start(bf16[64,24,128]{2,1,0:T(8,128)(2,1)} %stack.20), calls=%async_computation.2 | async-start | bytes 786432 | tf_op jit(solution)/shard_map/all_to_all | solution.py:12
  359.4 1.5 fusion.16
  364.3 74.5 %all-reduce.23.cloned.1.call-done = bf16[128,384]{0,1:T(8,128)(2,1)} async-done(((bf16[128,384]{0,1:T(8,128)(2,1)}), bf16[128,384]{0,1:T(8,128)(2,1)}) %all-reduce.23.cloned.1.call-update) | async-done | bytes 98320 | tf_op jit(solution)/shard_map/psum | solution.py:38
  438.8 1.8 fusion.23
  441.8 75.2 %all-reduce.37.cloned.1.call-done = (bf16[128,384]{0,1:T(8,128)(2,1)}, bf16[128,384]{0,1:T(8,128)(2,1)}) async-done(((bf16[128,384]{0,1:T(8,128)(2,1)}, bf16[128,384]{0,1:T(8,128)(2,1)}), (bf16[128,384]{0,1:T(8,128)(2,1)}, bf16[128,384]{0,1:T(8,128)(2,1)})) %all-reduce.37.cloned.1.call-update) | async-done | bytes 196624 | tf_op jit(solution)/shard_map/psum | solution.py:18
  518.1 1.9 scatter_fusion.2
  521.5 11.1 %all-to-all-start.3 = ((bf16[64,24,128]{2,1,0:T(8,128)(2,1)}), bf16[64,24,128]{2,1,0:T(8,128)(2,1)}, u32[]{:S(2)}, u32[]{:S(2)}) async-start(bf16[64,24,128]{2,1,0:T(8,128)(2,1)} %stack.21), calls=%async_computation.3 | async-start | bytes 786432 | tf_op jit(solution)/shard_map/all_to_all | solution.py:12
  537.5 74.6 %all-reduce.25.cloned.1.call-done = bf16[128,384]{0,1:T(8,128)(2,1)} async-done(((bf16[128,384]{0,1:T(8,128)(2,1)}), bf16[128,384]{0,1:T(8,128)(2,1)}) %all-reduce.25.cloned.1.call-update) | async-done | bytes 98320 | tf_op jit(solution)/shard_map/psum | solution.py:38
  612.1 1.8 fusion.25
  615.1 75.4 %all-reduce.35.cloned.1.call-done = (bf16[128,384]{0,1:T(8,128)(2,1)}, bf16[128,384]{0,1:T(8,128)(2,1)}) async-done(((bf16[128,384]{0,1:T(8,128)(2,1)}, bf16[128,384]{0,1:T(8,128)(2,1)}), (bf16[128,384]{0,1:T(8,128)(2,1)}, bf16[128,384]{0,1:T(8,128)(2,1)})) %all-reduce.35.cloned.1.call-update) | async-done | bytes 196624 | tf_op jit(solution)/shard_map/psum | solution.py:18
  691.5 1.7 scatter_fusion.3
  694.7 11.1 %all-to-all-start.4 = ((bf16[64,24,128]{2,1,0:T(8,128)(2,1)}), bf16[64,24,128]{2,1,0:T(8,128)(2,1)}, u32[]{:S(2)}, u32[]{:S(2)}) async-start(bf16[64,24,128]{2,1,0:T(8,128)(2,1)} %stack.22), calls=%async_computation.4 | async-start | bytes 786432 | tf_op jit(solution)/shard_map/all_to_all | solution.py:12
  710.8 74.6 %all-reduce.27.cloned.1.call-done = bf16[128,384]{0,1:T(8,128)(2,1)} async-done(((bf16[128,384]{0,1:T(8,128)(2,1)}), bf16[128,384]{0,1:T(8,128)(2,1)}) %all-reduce.27.cloned.1.call-update) | async-done | bytes 98320 | tf_op jit(solution)/shard_map/psum | solution.py:38
  785.4 1.8 fusion.27
  787.2 76.4 %all-reduce.33.cloned.1.call-done = (bf16[128,384]{0,1:T(8,128)(2,1)}, bf16[128,384]{0,1:T(8,128)(2,1)}) async-done(((bf16[128,384]{0,1:T(8,128)(2,1)}, bf16[128,384]{0,1:T(8,128)(2,1)}), (bf16[128,384]{0,1:T(8,128)(2,1)}, bf16[128,384]{0,1:T(8,128)(2,1)})) %all-reduce.33.cloned.1.call-update) | async-done | bytes 196624 | tf_op jit(solution)/shard_map/psum | solution.py:18
  864.6 1.7 scatter_fusion.4
  867.8 11.1 %all-to-all-start.5 = ((bf16[64,24,128]{2,1,0:T(8,128)(2,1)}), bf16[64,24,128]{2,1,0:T(8,128)(2,1)}, u32[]{:S(2)}, u32[]{:S(2)}) async-start(bf16[64,24,128]{2,1,0:T(8,128)(2,1)} %stack.23), calls=%async_computation.5 | async-start | bytes 786432 | tf_op jit(solution)/shard_map/all_to_all | solution.py:12
  883.7 74.5 %all-reduce.29.cloned.1.call-done = bf16[128,384]{0,1:T(8,128)(2,1)} async-done(((bf16[128,384]{0,1:T(8,128)(2,1)}), bf16[128,384]{0,1:T(8,128)(2,1)}) %all-reduce.29.cloned.1.call-update) | async-done | bytes 98320 | tf_op jit(solution)/shard_map/psum | solution.py:38
  958.2 1.8 fusion.29
  960.1 76.4 %all-reduce.31.cloned.1.call-done = (bf16[128,384]{0,1:T(8,128)(2,1)}, bf16[128,384]{0,1:T(8,128)(2,1)}) async-done(((bf16[128,384]{0,1:T(8,128)(2,1)}, bf16[128,384]{0,1:T(8,128)(2,1)}), (bf16[128,384]{0,1:T(8,128)(2,1)}, bf16[128,384]{0,1:T(8,128)(2,1)})) %all-reduce.31.cloned.1.call-update) | async-done | bytes 196624 | tf_op jit(solution)/shard_map/psum | solution.py:18
  1037.5 1.7 scatter_fusion.5
  (175 shorter events, 50.1 us)
Async XLA Ops:
  6.5 86.0 %all-reduce.19.cloned.1.call-start = ((), (), s32[]{:S(2)}) async-start(), calls=%async_computation.6 | async-start | bytes 196608 | tf_op jit(solution)/shard_map/psum | solution.py:38
  12.1 162.2 %all-to-all-start = ((bf16[64,24,128]{2,1,0:T(8,128)(2,1)}), bf16[64,24,128]{2,1,0:T(8,128)(2,1)S(1)}, u32[]{:S(2)}, u32[]{:S(2)}) async-start(bf16[64,24,128]{2,1,0:T(8,128)(2,1)} %stack.18), calls=%async_computation | async-start | bytes 786432 | tf_op jit(solution)/shard_map/all_to_all | solution.py:12
  26.0 144.9 %all-reduce.41.cloned.1.call-start = ((), (), s32[]{:S(2)}) async-start(), calls=%async_computation.17 | async-start | bytes 393216 | tf_op jit(solution)/shard_map/psum | solution.py:18
  174.3 12.0 %copy-start.1 = (bf16[128,384]{0,1:T(8,128)(2,1)S(1)}, bf16[128,384]{0,1:T(8,128)(2,1)}, u32[]{:S(2)}) copy-start(bf16[128,384]{0,1:T(8,128)(2,1)} %get-tuple-element.89) | copy-start | bytes 294916
  174.3 12.0 %copy-start.11 = (pred[1536]{0:T(1024)(128)(4,1)S(1)}, pred[1536]{0:T(1024)(128)(4,1)}, u32[]{:S(2)}) copy-start(pred[1536]{0:T(1024)(128)(4,1)} %fusion.48) | copy-start | bytes 4612
  175.2 172.3 %all-to-all-start.1 = ((bf16[64,24,128]{2,1,0:T(8,128)(2,1)}), bf16[64,24,128]{2,1,0:T(8,128)(2,1)}, u32[]{:S(2)}, u32[]{:S(2)}) async-start(bf16[64,24,128]{2,1,0:T(8,128)(2,1)} %stack.19), calls=%async_computation.1 | async-start | bytes 786432 | tf_op jit(solution)/shard_map/all_to_all | solution.py:12
  186.2 79.5 %all-reduce.21.cloned.1.call-start = ((), (), s32[]{:S(2)}) async-start(), calls=%async_computation.7 | async-start | bytes 196608 | tf_op jit(solution)/shard_map/psum | solution.py:38
  188.6 79.5 %copy-start.33 = (s32[128]{0:T(128)S(1)}, s32[128]{0:T(128)}, u32[]{:S(2)}) copy-start(s32[128]{0:T(128)} %get-tuple-element.119) | copy-start | bytes 1540
  188.7 156.3 %copy-start.29 = (s32[128]{0:T(128)S(1)}, s32[128]{0:T(128)}, u32[]{:S(2)}) copy-start(s32[128]{0:T(128)} %get-tuple-element.125) | copy-start | bytes 1540
  190.5 153.5 %all-reduce.39.cloned.1.call-start = ((), (), s32[]{:S(2)}) async-start(), calls=%async_computation.16 | async-start | bytes 393216 | tf_op jit(solution)/shard_map/psum | solution.py:18
  347.4 12.0 %copy-start.3 = (bf16[128,384]{0,1:T(8,128)(2,1)S(1)}, bf16[128,384]{0,1:T(8,128)(2,1)}, u32[]{:S(2)}) copy-start(bf16[128,384]{0,1:T(8,128)(2,1)} %get-tuple-element.87) | copy-start | bytes 294916
  348.2 172.4 %all-to-all-start.2 = ((bf16[64,24,128]{2,1,0:T(8,128)(2,1)}), bf16[64,24,128]{2,1,0:T(8,128)(2,1)}, u32[]{:S(2)}, u32[]{:S(2)}) async-start(bf16[64,24,128]{2,1,0:T(8,128)(2,1)} %stack.20), calls=%async_computation.2 | async-start | bytes 786432 | tf_op jit(solution)/shard_map/all_to_all | solution.py:12
  359.3 79.5 %all-reduce.23.cloned.1.call-start = ((), (), s32[]{:S(2)}) async-start(), calls=%async_computation.8 | async-start | bytes 196608 | tf_op jit(solution)/shard_map/psum | solution.py:38
  361.7 79.5 %copy-start.32 = (s32[128]{0:T(128)S(1)}, s32[128]{0:T(128)}, u32[]{:S(2)}) copy-start(s32[128]{0:T(128)} %get-tuple-element.117) | copy-start | bytes 1540
  361.7 156.3 %copy-start.27 = (s32[128]{0:T(128)S(1)}, s32[128]{0:T(128)}, u32[]{:S(2)}) copy-start(s32[128]{0:T(128)} %get-tuple-element.126) | copy-start | bytes 1540
  363.5 153.5 %all-reduce.37.cloned.1.call-start = ((), (), s32[]{:S(2)}) async-start(), calls=%async_computation.15 | async-start | bytes 393216 | tf_op jit(solution)/shard_map/psum | solution.py:18
  520.6 12.0 %copy-start.4 = (bf16[128,384]{0,1:T(8,128)(2,1)S(1)}, bf16[128,384]{0,1:T(8,128)(2,1)}, u32[]{:S(2)}) copy-start(bf16[128,384]{0,1:T(8,128)(2,1)} %get-tuple-element.85) | copy-start | bytes 294916
  520.7 12.0 %copy-start.13 = (pred[1536]{0:T(1024)(128)(4,1)S(1)}, pred[1536]{0:T(1024)(128)(4,1)}, u32[]{:S(2)}) copy-start(pred[1536]{0:T(1024)(128)(4,1)} %fusion.50) | copy-start | bytes 4612
  521.5 172.4 %all-to-all-start.3 = ((bf16[64,24,128]{2,1,0:T(8,128)(2,1)}), bf16[64,24,128]{2,1,0:T(8,128)(2,1)}, u32[]{:S(2)}, u32[]{:S(2)}) async-start(bf16[64,24,128]{2,1,0:T(8,128)(2,1)} %stack.21), calls=%async_computation.3 | async-start | bytes 786432 | tf_op jit(solution)/shard_map/all_to_all | solution.py:12
  532.6 79.5 %all-reduce.25.cloned.1.call-start = ((), (), s32[]{:S(2)}) async-start(), calls=%async_computation.9 | async-start | bytes 196608 | tf_op jit(solution)/shard_map/psum | solution.py:38
  534.9 79.6 %copy-start.31 = (s32[128]{0:T(128)S(1)}, s32[128]{0:T(128)}, u32[]{:S(2)}) copy-start(s32[128]{0:T(128)} %get-tuple-element.115) | copy-start | bytes 1540
  535.0 156.5 %copy-start.25 = (s32[128]{0:T(128)S(1)}, s32[128]{0:T(128)}, u32[]{:S(2)}) copy-start(s32[128]{0:T(128)} %get-tuple-element.127) | copy-start | bytes 1540
  536.8 153.7 %all-reduce.35.cloned.1.call-start = ((), (), s32[]{:S(2)}) async-start(), calls=%async_computation.14 | async-start | bytes 393216 | tf_op jit(solution)/shard_map/psum | solution.py:18
  694.7 172.3 %all-to-all-start.4 = ((bf16[64,24,128]{2,1,0:T(8,128)(2,1)}), bf16[64,24,128]{2,1,0:T(8,128)(2,1)}, u32[]{:S(2)}, u32[]{:S(2)}) async-start(bf16[64,24,128]{2,1,0:T(8,128)(2,1)} %stack.22), calls=%async_computation.4 | async-start | bytes 786432 | tf_op jit(solution)/shard_map/all_to_all | solution.py:12
  705.8 79.5 %all-reduce.27.cloned.1.call-start = ((), (), s32[]{:S(2)}) async-start(), calls=%async_computation.10 | async-start | bytes 196608 | tf_op jit(solution)/shard_map/psum | solution.py:38
  708.2 79.0 %copy-start.30 = (s32[128]{0:T(128)S(1)}, s32[128]{0:T(128)}, u32[]{:S(2)}) copy-start(s32[128]{0:T(128)} %get-tuple-element.91) | copy-start | bytes 1540
  708.2 156.4 %copy-start.23 = (s32[128]{0:T(128)S(1)}, s32[128]{0:T(128)}, u32[]{:S(2)}) copy-start(s32[128]{0:T(128)} %get-tuple-element.128) | copy-start | bytes 1540
  710.0 153.5 %all-reduce.33.cloned.1.call-start = ((), (), s32[]{:S(2)}) async-start(), calls=%async_computation.13 | async-start | bytes 393216 | tf_op jit(solution)/shard_map/psum | solution.py:18
  867.8 172.1 %all-to-all-start.5 = ((bf16[64,24,128]{2,1,0:T(8,128)(2,1)}), bf16[64,24,128]{2,1,0:T(8,128)(2,1)}, u32[]{:S(2)}, u32[]{:S(2)}) async-start(bf16[64,24,128]{2,1,0:T(8,128)(2,1)} %stack.23), calls=%async_computation.5 | async-start | bytes 786432 | tf_op jit(solution)/shard_map/all_to_all | solution.py:12
  878.9 79.3 %all-reduce.29.cloned.1.call-start = ((), (), s32[]{:S(2)}) async-start(), calls=%async_computation.11 | async-start | bytes 196608 | tf_op jit(solution)/shard_map/psum | solution.py:38
  881.3 156.2 %copy-start.21 = (s32[128]{0:T(128)S(1)}, s32[128]{0:T(128)}, u32[]{:S(2)}) copy-start(s32[128]{0:T(128)} %get-tuple-element.124) | copy-start | bytes 1540
  883.0 153.5 %all-reduce.31.cloned.1.call-start = ((), (), s32[]{:S(2)}) async-start(), calls=%async_computation.12 | async-start | bytes 393216 | tf_op jit(solution)/shard_map/psum | solution.py:18
  (20 other events, 85.0 us)
Sparse Core Ops, SparseCore 0:
  10.8 81.6 all-reduce.18
  95.0 75.9 all-reduce.40
  190.6 75.0 all-reduce.20
  268.0 75.9 all-reduce.38
  363.7 75.0 all-reduce.22
  441.1 75.9 all-reduce.36
  536.9 75.1 all-reduce.24
  614.5 75.9 all-reduce.34
  710.2 75.1 all-reduce.26
  787.6 75.9 all-reduce.32
  883.1 75.0 all-reduce.28
  960.5 75.9 all-reduce.30
